TPU v7x, 32 devices: a whole 2x2x4 slice. The times are simulated.
32 devices in a mesh: groups: 2 (over y), rows: 4 (over z), mp: 2 (over x), pair: 2 (over core).
Axes of the slice: x: 2, y: 2, z: 4, core: 2. Of those that a mesh axis runs over, the one named last changes fastest.
Arguments:
- query_rows: bfloat16 [2048, 512], P(('groups', 'rows', 'pair'), 'mp'), parts along dimension 0, may hold values from -240 to 240
- key_rows: bfloat16 [65536, 512], P(('groups', 'rows', 'pair'), 'mp'), parts along dimension 0, may hold values from -24 to 24
- value_rows: bfloat16 [65536, 512], P(('groups', 'rows', 'pair'), 'mp'), parts along dimension 0, may hold values from -6 to 6
- cotangent: bfloat16 [2048, 512], P(('groups', 'rows', 'pair'), 'mp'), parts along dimension 0, may hold values from -1536 to 1536
- train_rows: int32 [16], P('groups'), parts along dimension 0, may hold values from 1 to 12288, as said below
- test_rows: int32 [16], P('groups'), parts along dimension 0, may hold values from 32 to 128
- block_table: int32 [128], P('groups'), parts along dimension 0, may hold values from 0 to 7, as said below
Outputs:
- query_grad: bfloat16 [2048, 512], P(('groups', 'rows', 'pair'), 'mp'), parts along dimension 0
- key_grad: bfloat16 [65536, 512], P(('groups', 'rows', 'pair'), 'mp'), parts along dimension 0
- value_grad: bfloat16 [65536, 512], P(('groups', 'rows', 'pair'), 'mp'), parts along dimension 0
There are 2 independent parts, one for each index of `groups`. A program takes and returns all parts, laid end to end along the dimension named above; each array names one. Nothing has to cross between parts.
Inputs may be any that keep to these rules, and one draw needn't show every extreme that they name: block_table names table t exactly ceil(train_rows[t] / 512) times; the largest table has 24 full blocks. `block_table`: every table is named at least once.
All inputs are finite; a program needn't handle non-finite values.
Results may differ from a plain program's by a relative error of at most 0.0075.
Values may be sent and summed in bfloat16 or wider, within the bound.
No kernel may reach another device: no remote copies, remote signals or barrier semaphores. Data moves between devices by JAX's collectives and lax.ppermute only.
A program may use at most 64 MiB of HBM per device.

v0:
```python
import math
import jax
import jax.numpy as jnp
from jax import lax
from jax.sharding import PartitionSpec as P

HD = 64
TEST = 128
BLK = 512
NEG = -1e30


def combined_all(value, axis, join):
    pieces = jax.tree.map(lambda part: lax.all_gather(part, axis), value)
    head = jax.tree.map(lambda part: part[0], pieces)
    tail = jax.tree.map(lambda part: part[1:], pieces)
    total, _ = lax.scan(lambda total, piece: (join(total, piece), None), head, tail)
    return total


def table_lookup(positions, entries):
    matches = positions[:, None] == jnp.arange(entries.shape[0], dtype=jnp.int32)[None, :]
    return jnp.sum(jnp.where(matches, entries[None, :], 0), axis=1)


def merge_two(former, latter):
    new_peak = jnp.maximum(former[0], latter[0])
    return (
        new_peak,
        former[1] * jnp.exp(former[0] - new_peak) + latter[1] * jnp.exp(latter[0] - new_peak),
    )


def contract_rows(left, right):
    return lax.dot_general(
        left, right, (((0,), (0,)), ((), ())), preferred_element_type=jnp.float32
    )


def contract_features(left, right):
    return lax.dot_general(
        left, right, (((1,), (1,)), ((), ())), preferred_element_type=jnp.float32
    )


def local(query_rows, key_rows, value_rows, cotangent, train_rows, test_rows, block_table):
    device = lax.axis_index(("rows", "pair"))
    local_rows = query_rows.shape[0]
    features = query_rows.shape[1]
    head_count = features // HD
    blocks = key_rows.shape[0] // BLK
    tables = train_rows.shape[0]
    query_count = tables * TEST
    stacked = head_count * TEST
    score_scale = 1.0 / math.sqrt(HD)
    row_ids = device * local_rows + jnp.arange(local_rows, dtype=jnp.int32)
    query_live = row_ids % TEST < table_lookup(row_ids // TEST, test_rows)
    live_grads = jnp.where(query_live[:, None], cotangent, jnp.zeros_like(cotangent))
    all_queries, all_grads = (
        lax.all_gather(query_rows, ("rows", "pair"), axis=0, tiled=True),
        lax.all_gather(live_grads, ("rows", "pair"), axis=0, tiled=True),
    )
    head_of_feature = jnp.arange(features, dtype=jnp.int32) // HD
    head_mask = head_of_feature[None, :] == jnp.arange(head_count, dtype=jnp.int32)[:, None]

    def expand(rows):
        shaped = rows.reshape(tables, 1, TEST, features)
        masked = jnp.where(head_mask[None, :, None, :], shaped, jnp.zeros_like(shaped))
        return masked.reshape(tables, stacked, features)

    def collapse(product):
        shaped = product.reshape(head_count, TEST, features)
        return jnp.sum(jnp.where(head_mask[:, None, :], shaped, 0.0), axis=0)

    spread_queries = expand(all_queries)
    spread_grads = expand(all_grads)
    block_ids = jnp.arange(block_table.shape[0], dtype=jnp.int32)
    my_blocks = device * blocks + jnp.arange(blocks, dtype=jnp.int32)
    block_owner = lax.dynamic_slice_in_dim(block_table, device * blocks, blocks)
    earlier = (block_table[None, :] == block_owner[:, None]) & (
        block_ids[None, :] < my_blocks[:, None]
    )
    ordinal = jnp.sum(jnp.where(earlier, 1, 0), axis=1).astype(jnp.int32)
    live_keys = table_lookup(block_owner, train_rows) - ordinal * BLK
    key_blocks = key_rows.reshape(blocks, BLK, features)
    value_blocks = value_rows.reshape(blocks, BLK, features)
    key_index = jnp.arange(BLK, dtype=jnp.int32)
    block_inputs = (block_owner, live_keys, key_blocks, value_blocks)

    def block_scores(which_table, live_count, key_block):
        query_block = spread_queries[which_table]
        raw_scores = contract_features(query_block, key_block) * score_scale
        return (query_block, jnp.where(key_index[None, :] < live_count, raw_scores, NEG))

    def stats_step(running, inputs):
        which_table, live_count, key_block, value_block = inputs
        _, scores = block_scores(which_table, live_count, key_block)
        block_peak = jnp.max(scores, axis=1)
        weights = jnp.exp(scores - block_peak[:, None])
        block_mass = jnp.sum(weights, axis=1)
        old_peak = running[0][which_table]
        old_mass = running[1][which_table]
        new_peak = jnp.maximum(old_peak, block_peak)
        old_weight = jnp.exp(old_peak - new_peak)
        new_weight = jnp.exp(block_peak - new_peak)
        updated = [
            running[0].at[which_table].set(new_peak),
            running[1].at[which_table].set(old_mass * old_weight + block_mass * new_weight),
        ]
        return (tuple(updated), None)

    initial = [
        jnp.full((tables, stacked), NEG, jnp.float32),
        jnp.zeros((tables, stacked), jnp.float32),
    ]
    result, _ = lax.scan(stats_step, tuple(initial), block_inputs)
    peaks, masses = result
    peaks, masses = combined_all((peaks, masses), ("rows", "pair"), merge_two)

    def inner_step(running, inputs):
        which_table, live_count, key_block, value_block = inputs
        _, scores = block_scores(which_table, live_count, key_block)
        dprobs = contract_features(spread_grads[which_table], value_block)
        block_peak = jnp.max(scores, axis=1)
        weights_low = jnp.exp(scores - block_peak[:, None]).astype(jnp.bfloat16).astype(jnp.float32)
        term = (
            jnp.sum(weights_low * dprobs, axis=1)
            * jnp.exp(block_peak - peaks[which_table])
            / masses[which_table]
        )
        return (running.at[which_table].add(term), None)

    inner_terms, _ = lax.scan(inner_step, jnp.zeros((tables, stacked), jnp.float32), block_inputs)
    inner = lax.psum(inner_terms, ("rows", "pair"))

    def grad_step(running, inputs):
        which_table, live_count, key_block, value_block = inputs
        query_block, scores = block_scores(which_table, live_count, key_block)
        grad_block = spread_grads[which_table]
        probs = jnp.exp(scores - peaks[which_table][:, None]) / masses[which_table][:, None]
        dprobs = contract_features(grad_block, value_block)
        probs_low = probs.astype(jnp.bfloat16)
        value_part = contract_rows(probs_low, grad_block)
        dscores = (probs * (dprobs - inner[which_table][:, None])).astype(jnp.bfloat16)
        key_part = contract_rows(dscores, query_block) * score_scale
        query_part = (
            collapse(jnp.dot(dscores, key_block, preferred_element_type=jnp.float32)) * score_scale
        )
        running = running.at[which_table].add(query_part)
        return (running, (key_part.astype(jnp.bfloat16), value_part.astype(jnp.bfloat16)))

    query_terms, (key_parts, value_parts) = lax.scan(
        grad_step, jnp.zeros((tables, TEST, features), jnp.float32), block_inputs
    )
    query_total = lax.psum_scatter(
        query_terms.reshape(query_count, features),
        ("rows", "pair"),
        scatter_dimension=0,
        tiled=True,
    )
    return (
        query_total.astype(jnp.bfloat16),
        key_parts.reshape(blocks * BLK, features),
        value_parts.reshape(blocks * BLK, features),
    )


def solution(mesh):
    in_specs = (
        P(("groups", "rows", "pair"), "mp"),
        P(("groups", "rows", "pair"), "mp"),
        P(("groups", "rows", "pair"), "mp"),
        P(("groups", "rows", "pair"), "mp"),
        P("groups"),
        P("groups"),
        P("groups"),
    )
    out_specs = (
        P(("groups", "rows", "pair"), "mp"),
        P(("groups", "rows", "pair"), "mp"),
        P(("groups", "rows", "pair"), "mp"),
    )
    return jax.shard_map(local, mesh=mesh, in_specs=in_specs, out_specs=out_specs, check_vma=False)
```

profile of v0, /device:TPU:0, one launch (start us, length us, event | category | flops | bytes accessed | tf_op | source)
XLA Modules:
  0.0 357.1 jit_solution(11898617688526695184)
XLA Ops:
  11.4 16.6 %all_gather.23 = bf16[1024,256]{1,0:T(8,128)(2,1)S(1)} all-gather(bf16[128,256]{1,0:T(8,128)(2,1)S(1)} %broadcast_select_fusion.3), channel_id=1, replica_groups=mesh['groups'=2,'rows'=4,'mp'=2,'pair'=2] {'rows','pair'}, dimensions={0}, use_global_device_ids=true | all-gather | bytes 589824 | tf_op jit(solution)/shard_map/all_gather | solution.py:61
  28.0 14.9 %all_gather.18 = bf16[1024,256]{1,0:T(8,128)(2,1)S(1)} all-gather(bf16[128,256]{1,0:T(8,128)(2,1)} %param.23), channel_id=1, replica_groups=mesh['groups'=2,'rows'=4,'mp'=2,'pair'=2] {'rows','pair'}, dimensions={0}, use_global_device_ids=true | all-gather | bytes 589824 | tf_op jit(solution)/shard_map/all_gather | solution.py:60
  42.9 1.7 bitcast_select_fusion
  44.6 55.1 %while.60 = (s32[]{:T(128)}, f32[8,512]{1,0:T(8,128)S(1)}, f32[8,512]{1,0:T(8,128)S(1)}, s32[8]{0:T(128)S(1)}, s32[8]{0:T(128)S(1)}, /*index=5*/bf16[8,512,256]{...) while((s32[]{:T(128)}, f32[8,512]{1,0:T(8,128)S(1)}, ...), condition=%wide.region_7.8_spmd.clone.clone, body=%wide.region_3.7_spmd.clone.sunk.clone | while | flops 135532048 | bytes 2649797 | solution.py:116
  99.8 14.2 %all-gather.1 = f32[64,512]{1,0:T(8,128)S(1)} all-gather(f32[8,512]{1,0:T(8,128)S(1)} %get-tuple-element.259), channel_id=3, replica_groups=mesh['groups'=2,'rows'=4,'mp'=2,'pair'=2] {'rows','pair'}, dimensions={0}, use_global_device_ids=true | all-gather | bytes 147456 | tf_op jit(solution)/shard_map/all_gather | solution.py:14
  114.0 14.0 %all-gather = f32[64,512]{1,0:T(8,128)S(1)} all-gather(f32[8,512]{1,0:T(8,128)S(1)} %get-tuple-element.258), channel_id=2, replica_groups=mesh['groups'=2,'rows'=4,'mp'=2,'pair'=2] {'rows','pair'}, dimensions={0}, use_global_device_ids=true | all-gather | bytes 147456 | tf_op jit(solution)/shard_map/all_gather | solution.py:14
  128.3 61.7 %while.61 = (s32[]{:T(128)}, f32[8,512]{1,0:T(8,128)S(1)}, s32[8]{0:T(128)S(1)}, s32[8]{0:T(128)S(1)}, bf16[8,512,256]{2,1,0:T(8,128)(2,1)}, /*index=5*/bf16[8,5...) while((s32[]{:T(128)}, f32[8,512]{1,0:T(8,128)S(1)}, ...), condition=%wide.region_14.15_spmd.clone.clone, body=%wide.region_10.14_spmd.clone.sunk.clone | while | flops 270534656 | bytes 3170525 | solution.py:133
  190.1 29.2 %psum.7 = f32[8,512]{1,0:T(8,128)S(1)} all-reduce(f32[8,512]{1,0:T(8,128)S(1)} %get-tuple-element.262), channel_id=1, replica_groups=mesh['groups'=2,'rows'=4,'mp'=2,'pair'=2] {'rows','pair'}, use_global_device_ids=true, to_apply=%region_15.16 | all-reduce | flops 4096 | bytes 32768 | tf_op jit(solution)/shard_map/psum | solution.py:134
  219.4 97.7 %while.62 = (s32[]{:T(128)}, f32[8,128,256]{2,1,0:T(8,128)S(1)}, bf16[8,512,256]{2,1,0:T(8,128)(2,1)}, bf16[8,512,256]{2,1,0:T(8,128)(2,1)}, s32[8]{0:T(128)S(1)...) while((s32[]{:T(128)}, f32[8,128,256]{2,1,0:T(8,128)S(1)}, ...), condition=%wide.region_19.20_spmd.clone.clone, body=%wide.region_16.19_spmd.clone.sunk.clone | while | flops 673908224 | bytes 7627025 | solution.py:152
  229.6 2.0 fusion.131
  236.0 1.5 fusion.127
  241.8 2.0 fusion.131
  248.3 1.5 fusion.127
  254.0 2.0 fusion.131
  260.5 1.5 fusion.127
  266.2 2.0 fusion.131
  272.7 1.5 fusion.127
  278.4 2.0 fusion.131
  284.9 1.5 fusion.127
  290.6 2.0 fusion.131
  302.9 2.0 fusion.131
  315.1 2.0 fusion.131
  318.1 30.6 %reduce-scatter.2.cloned.1.call-done = f32[128,256]{1,0:T(8,128)} async-done(((f32[1024,256]{1,0:T(8,128)}), f32[128,256]{1,0:T(8,128)}) %reduce-scatter.2.cloned.1.call-update) | async-done | bytes 131088 | tf_op jit(solution)/shard_map/reduce_scatter | solution.py:155
  348.7 1.5 convert_element_type.21
  (265 shorter events, 151.3 us)
Async XLA Ops:
  7.2 341.5 %reduce-scatter.2.cloned.1.call-start = ((), (), s32[]{:S(2)}) async-start(), calls=%async_computation.1 | async-start | bytes 1179648 | tf_op jit(solution)/shard_map/reduce_scatter | solution.py:155
  42.9 1.7 copy-start.1
  128.3 91.1 %copy-start.2 = (s32[3]{0:T(128)S(1)}, s32[3]{0:T(128)}, u32[]{:S(2)}) copy-start(s32[3]{0:T(128)} %constant.200.clone.2) | copy-start | bytes 40
  317.1 1.0 copy-start
Sparse Core Ops, SparseCore 0:
  318.2 30.4 reduce-scatter.1
where the time goes:
time: 360 us; the launch traced here: 357 us
  matrix products  89.4 us (25%)
  blocking collectives  89 us (25%)
  other arithmetic  55.6 us (15%)
  loops' own time  45.8 us (13%)
  local copies, waits for them, and re-layouts  32.5 us (9%)
  waiting for transfers between devices  30.6 us (8%)
  between operations  14.2 us (4%)
    dot_general x40, matrix products, contract_features(): lax.dot_general(left, right, (((1,), (1,)), ((), ())), preferred_element_...  54.7 us
    reduce_scatter x1, waiting for transfers between devices, local(): lax.psum_scatter(query_terms.reshape(query_count, features), ('rows', 'pa...  30.6 us
    psum x1, blocking collectives, local(): inner = lax.psum(inner_terms, ('rows', 'pair'))  29.2 us
    dynamic_slice x48, local copies, waits for them, and re-layouts, local(): result, _ = lax.scan(stats_step, tuple(initial), block_inputs)  29 us
    all_gather x2, blocking collectives, combined_all(): pieces = jax.tree.map(lambda part: lax.all_gather(part, axis), value)  28.2 us
    another operation x42, other arithmetic  27.8 us
    dot_general x16, matrix products, contract_rows(): lax.dot_general(left, right, (((0,), (0,)), ((), ())), preferred_element_...  24.6 us
    all_gather x1, blocking collectives, local(): lax.all_gather(live_grads, ('rows', 'pair'), axis=0, tiled=True)  16.6 us
  transfers between devices with their start and end apart: 1, of which 1 were waited for; matrix products, arithmetic and copies ran while one was open for 0% of the time, Pallas kernels for 0%

commit v1 on v0

--- a/solution.py
+++ b/solution.py
@@ -131,7 +131,7 @@
         return (running.at[which_table].add(term), None)
 
     inner_terms, _ = lax.scan(inner_step, jnp.zeros((tables, stacked), jnp.float32), block_inputs)
-    inner = lax.psum(inner_terms, ("rows", "pair"))
+    inner = lax.psum(lax.psum(inner_terms, "pair"), "rows")
 
     def grad_step(running, inputs):
         which_table, live_count, key_block, value_block = inputs

time: 360 us -> 353 us (0.981)
  blocking collectives: 89 us -> 82.1 us
    psum x1 -> x2, blocking collectives: 29.2 us -> 22.4 us  [local(): inner = lax.psum(lax.psum(inner_terms, 'pair'), 'rows')]
where the time goes in v1:
time: 353 us; the launch traced here: 350 us
  matrix products  89.4 us (25%)
  blocking collectives  82.1 us (23%)
  other arithmetic  55.6 us (16%)
  loops' own time  45.8 us (13%)
  local copies, waits for them, and re-layouts  32.5 us (9%)
  waiting for transfers between devices  30.6 us (9%)
  between operations  14.2 us (4%)
    dot_general x40, matrix products, contract_features(): lax.dot_general(left, right, (((1,), (1,)), ((), ())), preferred_element_...  54.7 us
    reduce_scatter x1, waiting for transfers between devices, local(): lax.psum_scatter(query_terms.reshape(query_count, features), ('rows', 'pa...  30.6 us
    dynamic_slice x48, local copies, waits for them, and re-layouts, local(): result, _ = lax.scan(stats_step, tuple(initial), block_inputs)  29 us
    all_gather x2, blocking collectives, combined_all(): pieces = jax.tree.map(lambda part: lax.all_gather(part, axis), value)  28.2 us
    another operation x42, other arithmetic  27.8 us
    dot_general x16, matrix products, contract_rows(): lax.dot_general(left, right, (((0,), (0,)), ((), ())), preferred_element_...  24.6 us
    psum x2, blocking collectives, local(): inner = lax.psum(lax.psum(inner_terms, 'pair'), 'rows')  22.4 us
    all_gather x1, blocking collectives, local(): lax.all_gather(live_grads, ('rows', 'pair'), axis=0, tiled=True)  16.6 us
  transfers between devices with their start and end apart: 1, of which 1 were waited for; matrix products, arithmetic and copies ran while one was open for 0% of the time, Pallas kernels for 0%

profile of v1, /device:TPU:0, one launch (start us, length us, event | category | flops | bytes accessed | tf_op | source)
XLA Modules:
  0.0 350.3 jit_solution(12596269542864273355)
XLA Ops:
  11.4 16.6 %all_gather.23 = bf16[1024,256]{1,0:T(8,128)(2,1)S(1)} all-gather(bf16[128,256]{1,0:T(8,128)(2,1)S(1)} %broadcast_select_fusion.3), channel_id=1, replica_groups=mesh['groups'=2,'rows'=4,'mp'=2,'pair'=2] {'rows','pair'}, dimensions={0}, use_global_device_ids=true | all-gather | bytes 589824 | tf_op jit(solution)/shard_map/all_gather | solution.py:61
  28.0 14.9 %all_gather.18 = bf16[1024,256]{1,0:T(8,128)(2,1)S(1)} all-gather(bf16[128,256]{1,0:T(8,128)(2,1)} %param.23), channel_id=1, replica_groups=mesh['groups'=2,'rows'=4,'mp'=2,'pair'=2] {'rows','pair'}, dimensions={0}, use_global_device_ids=true | all-gather | bytes 589824 | tf_op jit(solution)/shard_map/all_gather | solution.py:60
  42.9 1.7 bitcast_select_fusion
  44.6 55.1 %while.60 = (s32[]{:T(128)}, f32[8,512]{1,0:T(8,128)S(1)}, f32[8,512]{1,0:T(8,128)S(1)}, s32[8]{0:T(128)S(1)}, s32[8]{0:T(128)S(1)}, /*index=5*/bf16[8,512,256]{...) while((s32[]{:T(128)}, f32[8,512]{1,0:T(8,128)S(1)}, ...), condition=%wide.region_7.8_spmd.clone.clone, body=%wide.region_3.7_spmd.clone.sunk.clone | while | flops 135532048 | bytes 2649797 | solution.py:116
  99.8 14.2 %all-gather.1 = f32[64,512]{1,0:T(8,128)S(1)} all-gather(f32[8,512]{1,0:T(8,128)S(1)} %get-tuple-element.259), channel_id=3, replica_groups=mesh['groups'=2,'rows'=4,'mp'=2,'pair'=2] {'rows','pair'}, dimensions={0}, use_global_device_ids=true | all-gather | bytes 147456 | tf_op jit(solution)/shard_map/all_gather | solution.py:14
  114.0 14.0 %all-gather = f32[64,512]{1,0:T(8,128)S(1)} all-gather(f32[8,512]{1,0:T(8,128)S(1)} %get-tuple-element.258), channel_id=2, replica_groups=mesh['groups'=2,'rows'=4,'mp'=2,'pair'=2] {'rows','pair'}, dimensions={0}, use_global_device_ids=true | all-gather | bytes 147456 | tf_op jit(solution)/shard_map/all_gather | solution.py:14
  128.3 61.7 %while.61 = (s32[]{:T(128)}, f32[8,512]{1,0:T(8,128)S(1)}, s32[8]{0:T(128)S(1)}, s32[8]{0:T(128)S(1)}, bf16[8,512,256]{2,1,0:T(8,128)(2,1)}, /*index=5*/bf16[8,5...) while((s32[]{:T(128)}, f32[8,512]{1,0:T(8,128)S(1)}, ...), condition=%wide.region_14.15_spmd.clone.clone, body=%wide.region_10.14_spmd.clone.sunk.clone | while | flops 270534656 | bytes 3170525 | solution.py:133
  190.0 3.5 %psum.14 = f32[8,512]{1,0:T(8,128)S(1)} all-reduce(f32[8,512]{1,0:T(8,128)S(1)} %get-tuple-element.262), channel_id=1, replica_groups=mesh['groups'=2,'rows'=4,'mp'=2,'pair'=2] {'pair'}, use_global_device_ids=true, to_apply=%region_15.16 | all-reduce | flops 4096 | bytes 32768 | tf_op jit(solution)/shard_map/psum | solution.py:134
  193.6 18.9 %psum.15 = f32[8,512]{1,0:T(8,128)S(1)} all-reduce(f32[8,512]{1,0:T(8,128)S(1)} %psum.14), channel_id=1, replica_groups=mesh['groups'=2,'rows'=4,'mp'=2,'pair'=2] {'rows'}, use_global_device_ids=true, to_apply=%region_16.17 | all-reduce | flops 4096 | bytes 32768 | tf_op jit(solution)/shard_map/psum | solution.py:134
  212.6 97.7 %while.62 = (s32[]{:T(128)}, f32[8,128,256]{2,1,0:T(8,128)S(1)}, bf16[8,512,256]{2,1,0:T(8,128)(2,1)}, bf16[8,512,256]{2,1,0:T(8,128)(2,1)}, s32[8]{0:T(128)S(1)...) while((s32[]{:T(128)}, f32[8,128,256]{2,1,0:T(8,128)S(1)}, ...), condition=%wide.region_20.21_spmd.clone.clone, body=%wide.region_17.20_spmd.clone.sunk.clone | while | flops 673908224 | bytes 7627025 | solution.py:152
  217.0 1.5 fusion.127
  222.8 2.0 fusion.131
  235.0 2.0 fusion.131
  247.2 2.0 fusion.131
  253.7 1.5 fusion.127
  259.4 2.0 fusion.131
  265.9 1.5 fusion.127
  271.6 2.0 fusion.131
  283.9 2.0 fusion.131
  290.3 1.5 fusion.127
  296.1 2.0 fusion.131
  308.3 2.0 fusion.131
  311.3 30.6 %reduce-scatter.2.cloned.1.call-done = f32[128,256]{1,0:T(8,128)} async-done(((f32[1024,256]{1,0:T(8,128)}), f32[128,256]{1,0:T(8,128)}) %reduce-scatter.2.cloned.1.call-update) | async-done | bytes 131088 | tf_op jit(solution)/shard_map/reduce_scatter | solution.py:155
  341.9 1.5 convert_element_type.21
  (266 shorter events, 152.8 us)
Async XLA Ops:
  7.2 334.7 %reduce-scatter.2.cloned.1.call-start = ((), (), s32[]{:S(2)}) async-start(), calls=%async_computation.1 | async-start | bytes 1179648 | tf_op jit(solution)/shard_map/reduce_scatter | solution.py:155
  42.9 1.7 copy-start.1
  128.3 84.3 %copy-start.2 = (s32[3]{0:T(128)S(1)}, s32[3]{0:T(128)}, u32[]{:S(2)}) copy-start(s32[3]{0:T(128)} %constant.200.clone.2) | copy-start | bytes 40
  310.3 1.0 copy-start
Sparse Core Ops, SparseCore 0:
  311.4 30.4 reduce-scatter.1
